TPU v7x, 128 devices: a whole 4x4x4 slice. The times are simulated.
128 devices in a mesh: row: 16 (over z, x), vec: 8 (over y, core).
Axes of the slice: x: 4, y: 4, z: 4, core: 2. Of those that a mesh axis runs over, the one named last changes fastest.
Arguments:
- vectors: float32 [32768, 1024], P('row', 'vec'), may hold values from -8 to 8
- hamiltonian: float32 [256, 12, 128, 128], P('row'), may hold values from -0.15 to 0.15, as said below
- column_blocks: int32 [256, 12], P('row'), may hold values from 0 to 255, as said below
- live_counts: int32 [256], P('row'), may hold values from 3 to 12
- lower_bound: float32 [1], replicated, may hold values from -0.85 to -0.65
- upper_bound: float32 [1], replicated, may hold values from 1.05 to 1.3
Outputs:
- filtered: float32 [32768, 1024], P('row', 'vec')
Inputs may be any that keep to these rules, and one draw needn't show every extreme that they name: column_blocks[i, 0] = i, and every entry lies within 16 block rows of its row i, cyclically modulo 256; the distances 16 and -16 both occur. `hamiltonian`: H is symmetric: for every used slot of block row i that names column block j there is a used slot of block row j that names i and holds the transpose of its block, and slot 0 of every block row holds a symmetric block.
All inputs are finite; a program needn't handle non-finite values.
Results may differ from a plain program's by a relative error of at most 0.0003.
Values sent between devices are 32-bit elements; how exact they have to be, the bound alone decides.
No kernel may reach another device: no remote copies, remote signals or barrier semaphores. Data moves between devices by JAX's collectives and lax.ppermute only.
A program may use at most 128 MiB of HBM per device.

v0:
```python
import math
import jax
import jax.numpy as jnp
from jax import lax
from jax.sharding import PartitionSpec as P

NV = 1024
NS_ITERS = 3


def with_halo(cells, sides, width):
    for axis, dim in sides:
        count = lax.axis_size(axis)
        head = lax.slice_in_dim(cells, 0, width, axis=dim)
        tail = lax.slice_in_dim(cells, cells.shape[dim] - width, cells.shape[dim], axis=dim)
        cells = jnp.concatenate(
            [
                lax.ppermute(tail, axis, [(i, (i + 1) % count) for i in range(count)]),
                cells,
                lax.ppermute(head, axis, [((i + 1) % count, i) for i in range(count)]),
            ],
            axis=dim,
        )
    return cells


def on_device(vectors, hamiltonian, column_blocks, live_counts, lower_bound, upper_bound):
    rows_dev, panel_cols = vectors.shape
    block_rows, slot_count, block_size, unused_size = hamiltonian.shape
    row_count = lax.axis_size("row")
    first_row = lax.axis_index("row") * block_rows
    local_cols = (column_blocks - first_row + block_rows) % (block_rows * row_count)

    def apply_field(operand):
        widened = with_halo(operand, (("row", 0),), block_rows * block_size)
        widened_blocks = widened.reshape(3 * block_rows, block_size, panel_cols)
        picked = jnp.take(widened_blocks, local_cols, axis=0)
        live_mask = (
            jnp.arange(slot_count, dtype=jnp.int32)[None, :] < live_counts[:, None]
        ).astype(jnp.float32)
        summed = jnp.einsum(
            "rkij,rkjc->ric",
            hamiltonian,
            picked * live_mask[:, :, None, None],
            precision=lax.Precision.HIGHEST,
            preferred_element_type=jnp.float32,
        )
        return summed.reshape(rows_dev, panel_cols)

    centre = (upper_bound[0] + lower_bound[0]) / 2
    radius = (upper_bound[0] - lower_bound[0]) / 2
    first = (apply_field(vectors) - centre * vectors) / radius
    second = 2 * (apply_field(first) - centre * first) / radius - vectors
    energy = lax.psum(jnp.sum(second * second), ("row", "vec"))
    current = second * jnp.sqrt(NV / (4 * (energy + 1e-06)))
    stacked = current
    for iteration in range(NS_ITERS):
        stacked = lax.all_to_all(current, "vec", split_axis=0, concat_axis=1, tiled=True)
        local_gram = jnp.einsum(
            "rc,rd->cd",
            stacked,
            stacked,
            precision=lax.Precision.HIGHEST,
            preferred_element_type=jnp.float32,
        )
        gram = lax.psum(local_gram, ("row", "vec"))
        stacked = 1.5 * stacked - 0.5 * jnp.dot(
            stacked, gram, precision=lax.Precision.HIGHEST, preferred_element_type=jnp.float32
        )
        current = lax.all_to_all(stacked, "vec", split_axis=1, concat_axis=0, tiled=True)
    total_rows = rows_dev * row_count
    return current * math.sqrt(total_rows)


def solution(mesh):
    placed = (P("row", "vec"), P("row", None, None, None), P("row", None), P("row"), P(), P())
    return jax.shard_map(
        on_device, mesh=mesh, in_specs=placed, out_specs=P("row", "vec"), check_vma=False
    )
```

profile of v0, /device:TPU:1, one launch (start us, length us, event | category | flops | bytes accessed | tf_op | source)
XLA Modules:
  0.0 796.7 jit_solution(12494661973624520224)
XLA Ops:
  6.5 6.8 collective-permute-start.1
  15.5 20.0 %collective-permute-done.1 = f32[2048,128]{1,0:T(8,128)S(1)} collective-permute-done((f32[2048,128]{1,0:T(8,128)}, f32[2048,128]{1,0:T(8,128)S(1)}, u32[]{:S(2)}, u32[]{:S(2)}) %collective-permute-start.1) | collective-permute-done | bytes 1048608 | tf_op jit(solution)/shard_map/ppermute | solution.py:20
  42.8 5.9 gather_fusion
  48.7 19.3 %fusion.1 = f32[16,128,128,1]{1,2,3,0:T(8,128)S(1)} fusion(f32[16,12,128,128]{3,2,1,0:T(8,128)} %param.9, f32[16,12,128,128]{3,2,1,0:T(8,128)} %bitcast.112, f32[16,12]{1,0:T(8,128)S(1)} %get-tuple-element.10, pred[16,12]{1,0:T(8,128)(4,1)S(1)} %get-tuple-element.8), kind=kOutput, calls=%fused_computation.5 | convolution fusion | flops 4838129664 | bytes 26215360 | tf_op jit(solution)/shard_map/rkij,rkjc->ric/dot_general | solution.py:41
  69.7 21.4 %collective-permute-done.3 = f32[2048,128]{1,0:T(8,128)S(1)} collective-permute-done((f32[2048,128]{1,0:T(8,128)S(1)}, f32[2048,128]{1,0:T(8,128)S(1)}, u32[]{:S(2)}, u32[]{:S(2)}) %collective-permute-start.3) | collective-permute-done | bytes 1048608 | tf_op jit(solution)/shard_map/ppermute | solution.py:20
  91.1 4.5 collective-permute-done.2
  95.8 5.9 gather_fusion.1
  101.7 19.4 %fusion = f32[16,128,128,1]{1,2,3,0:T(8,128)S(1)} fusion(f32[16,12,128,128]{3,2,1,0:T(8,128)} %param.9, f32[16,12,128,128]{3,2,1,0:T(8,128)} %bitcast.111, f32[16,12]{1,0:T(8,128)S(1)} %get-tuple-element.10, pred[16,12]{1,0:T(8,128)(4,1)S(1)} %get-tuple-element.8), kind=kOutput, calls=%fused_computation.3 | convolution fusion | flops 4838129664 | bytes 26215360 | tf_op jit(solution)/shard_map/rkij,rkjc->ric/dot_general | solution.py:41
  122.1 65.0 %psum.28 = f32[]{:T(128)} all-reduce(f32[]{:T(128)} %get-tuple-element.6), channel_id=1, replica_groups=mesh['row'=16,'vec'=8] {'row','vec'}, use_global_device_ids=true, to_apply=%region_1.3 | all-reduce | flops 1 | bytes 8 | tf_op jit(solution)/shard_map/psum | solution.py:54
  187.9 19.4 %all_to_all.96 = f32[8,256,128]{2,1,0:T(8,128)S(1)} all-to-all(f32[8,256,128]{2,1,0:T(8,128)S(1)} %bitcast.113), channel_id=1, replica_groups=mesh['row'=16,'vec'=8] {'vec'}, dimensions={0} | all-to-all | bytes 2097152 | tf_op jit(solution)/shard_map/all_to_all | solution.py:58
  207.2 5.1 fusion.21
  212.4 150.4 %all-reduce.4.cloned.1.call-done = f32[1024,1024]{1,0:T(8,128)} async-done(((f32[1024,1024]{1,0:T(8,128)}), f32[1024,1024]{1,0:T(8,128)}) %all-reduce.4.cloned.1.call-update) | async-done | bytes 4194320 | tf_op jit(solution)/shard_map/psum | solution.py:66
  362.8 5.8 fusion.13
  368.7 19.7 %all_to_all.97 = f32[256,8,128]{2,0,1:T(8,128)S(1)} all-to-all(f32[256,8,128]{2,0,1:T(8,128)S(1)} %bitcast.114), channel_id=1, replica_groups=mesh['row'=16,'vec'=8] {'vec'}, dimensions={1} | all-to-all | bytes 2097152 | tf_op jit(solution)/shard_map/all_to_all | solution.py:70
  388.4 18.4 %all_to_all.98 = f32[8,256,128]{2,1,0:T(8,128)S(1)} all-to-all(f32[8,256,128]{2,1,0:T(8,128)S(1)} %bitcast.115), channel_id=1, replica_groups=mesh['row'=16,'vec'=8] {'vec'}, dimensions={0} | all-to-all | bytes 2097152 | tf_op jit(solution)/shard_map/all_to_all | solution.py:58
  406.8 5.1 fusion.18
  411.9 151.2 %all-reduce.6.cloned.1.call-done = f32[1024,1024]{1,0:T(8,128)} async-done(((f32[1024,1024]{1,0:T(8,128)}), f32[1024,1024]{1,0:T(8,128)}) %all-reduce.6.cloned.1.call-update) | async-done | bytes 4194320 | tf_op jit(solution)/shard_map/psum | solution.py:66
  563.1 5.8 fusion.11
  569.0 19.7 %all_to_all.99 = f32[256,8,128]{2,0,1:T(8,128)S(1)} all-to-all(f32[256,8,128]{2,0,1:T(8,128)S(1)} %bitcast.116), channel_id=1, replica_groups=mesh['row'=16,'vec'=8] {'vec'}, dimensions={1} | all-to-all | bytes 2097152 | tf_op jit(solution)/shard_map/all_to_all | solution.py:70
  588.7 18.4 %all_to_all.100 = f32[8,256,128]{2,1,0:T(8,128)S(1)} all-to-all(f32[8,256,128]{2,1,0:T(8,128)S(1)} %bitcast.117), channel_id=1, replica_groups=mesh['row'=16,'vec'=8] {'vec'}, dimensions={0} | all-to-all | bytes 2097152 | tf_op jit(solution)/shard_map/all_to_all | solution.py:58
  607.1 5.1 fusion.15
  612.2 151.4 %all-reduce.8.cloned.1.call-done = f32[1024,1024]{1,0:T(8,128)} async-done(((f32[1024,1024]{1,0:T(8,128)}), f32[1024,1024]{1,0:T(8,128)}) %all-reduce.8.cloned.1.call-update) | async-done | bytes 4194320 | tf_op jit(solution)/shard_map/psum | solution.py:66
  763.5 5.8 fusion.9
  769.4 19.7 %all_to_all.101 = f32[256,8,128]{2,0,1:T(8,128)S(1)} all-to-all(f32[256,8,128]{2,0,1:T(8,128)S(1)} %bitcast.118), channel_id=1, replica_groups=mesh['row'=16,'vec'=8] {'vec'}, dimensions={1} | all-to-all | bytes 2097152 | tf_op jit(solution)/shard_map/all_to_all | solution.py:70
  (32 shorter events, 12.5 us)
Async XLA Ops:
  6.5 356.3 %all-reduce.4.cloned.1.call-start = ((), (), s32[]{:S(2)}) async-start(), calls=%async_computation.6 | async-start | bytes 8388608 | tf_op jit(solution)/shard_map/psum | solution.py:66
  6.5 28.9 %collective-permute-start.1 = (f32[2048,128]{1,0:T(8,128)}, f32[2048,128]{1,0:T(8,128)S(1)}, u32[]{:S(2)}, u32[]{:S(2)}) collective-permute-start(f32[2048,128]{1,0:T(8,128)} %param.8), channel_id=1, source_target_pairs={{8,0},{16,8},{24,16},{32,24},{40,32},{48,40},{56,48},{64,56},{72,6... | collective-permute-start | bytes 3145736 | tf_op jit(solution)/shard_map/ppermute | solution.py:20
  13.3 27.4 %collective-permute-start = (f32[2048,128]{1,0:T(8,128)}, f32[2048,128]{1,0:T(8,128)}, u32[]{:S(2)}, u32[]{:S(2)}) collective-permute-start(f32[2048,128]{1,0:T(8,128)} %param.8), channel_id=1, source_target_pairs={{0,8},{8,16},{16,24},{24,32},{32,40},{40,48},{48,56},{56,64},{64,7... | collective-permute-start | bytes 3145736 | tf_op jit(solution)/shard_map/ppermute | solution.py:18
  35.5 1.0 copy-start.4
  48.7 19.3 %copy-start.2 = (f32[2048,128]{1,0:T(8,128)S(1)}, f32[2048,128]{1,0:T(8,128)}, u32[]{:S(2)}) copy-start(f32[2048,128]{1,0:T(8,128)} %param.8) | copy-start | bytes 3145732
  68.0 27.8 %copy-start = (f32[16,128,128,1]{1,2,3,0:T(8,128)}, f32[16,128,128,1]{1,2,3,0:T(8,128)S(1)}, u32[]{:S(2)}) copy-start(f32[16,128,128,1]{1,2,3,0:T(8,128)S(1)} %fusion.1) | copy-start | bytes 3145732
  68.1 23.0 %collective-permute-start.3 = (f32[2048,128]{1,0:T(8,128)S(1)}, f32[2048,128]{1,0:T(8,128)S(1)}, u32[]{:S(2)}, u32[]{:S(2)}) collective-permute-start(f32[2048,128]{1,0:T(8,128)S(1)} %fusion.26), channel_id=1, source_target_pairs={{8,0},{16,8},{24,16},{32,24},{40,32},{48,40},{56,48},{64,56},{72,6... | collective-permute-start | bytes 3145736 | tf_op jit(solution)/shard_map/ppermute | solution.py:20
  69.4 26.2 %collective-permute-start.2 = (f32[2048,128]{1,0:T(8,128)S(1)}, f32[2048,128]{1,0:T(8,128)S(1)}, u32[]{:S(2)}, u32[]{:S(2)}) collective-permute-start(f32[2048,128]{1,0:T(8,128)S(1)} %fusion.26), channel_id=1, source_target_pairs={{0,8},{8,16},{16,24},{24,32},{32,40},{40,48},{48,56},{56,64},{64,7... | collective-permute-start | bytes 3145736 | tf_op jit(solution)/shard_map/ppermute | solution.py:18
  101.7 19.4 %copy-start.1 = (f32[16,128,128,1]{1,2,3,0:T(8,128)S(1)}, f32[16,128,128,1]{1,2,3,0:T(8,128)}, u32[]{:S(2)}) copy-start(f32[16,128,128,1]{1,2,3,0:T(8,128)} %copy-done) | copy-start | bytes 3145732
  101.7 19.4 %copy-start.3 = (f32[2048,128]{1,0:T(8,128)S(1)}, f32[2048,128]{1,0:T(8,128)}, u32[]{:S(2)}) copy-start(f32[2048,128]{1,0:T(8,128)} %param.8) | copy-start | bytes 3145732
  212.3 350.8 %all-reduce.6.cloned.1.call-start = ((), (), s32[]{:S(2)}) async-start(), calls=%async_computation.7 | async-start | bytes 8388608 | tf_op jit(solution)/shard_map/psum | solution.py:66
  411.9 351.7 %all-reduce.8.cloned.1.call-start = ((), (), s32[]{:S(2)}) async-start(), calls=%async_computation.8 | async-start | bytes 8388608 | tf_op jit(solution)/shard_map/psum | solution.py:66
Sparse Core Ops, SparseCore 0:
  212.5 150.3 all-reduce.3
  412.0 151.0 all-reduce.5
  612.3 151.1 all-reduce.7
where the time goes:
time: 797 us
  waiting for transfers between devices  503 us (63%)
  blocking collectives  180 us (23%)
  matrix products  71.3 us (9%)
  between operations  15.3 us (2%)
  local copies, waits for them, and re-layouts  13.1 us (2%)
  starting transfers between devices  8.39 us (1%)
    psum x3, waiting for transfers between devices, on_device(): gram = lax.psum(local_gram, ('row', 'vec'))  453 us
    psum x1, blocking collectives, on_device(): energy = lax.psum(jnp.sum(second * second), ('row', 'vec'))  65 us
    all_to_all x3, blocking collectives, on_device(): lax.all_to_all(stacked, 'vec', split_axis=1, concat_axis=0, tiled=True)  59.1 us
    all_to_all x3, blocking collectives, on_device(): lax.all_to_all(current, 'vec', split_axis=0, concat_axis=1, tiled=True)  56.1 us
    ppermute x2, waiting for transfers between devices, with_halo(): lax.ppermute(head, axis, [((i + 1) % count, i) for i in range(count)])  41.4 us
    dot_general x2, matrix products, apply_field(): jnp.einsum('rkij,rkjc->ric', hamiltonian, picked * live_mask[:, :, None,...  38.7 us
    dot_general x3, matrix products, on_device(): jnp.dot(stacked, gram, precision=lax.Precision.HIGHEST, preferred_element...  17.4 us
  transfers between devices with their start and end apart: 7, of which 7 were waited for; matrix products, arithmetic and copies ran while one was open for 0% of the time, Pallas kernels for 0%

commit v1 on v0

--- a/solution.py
+++ b/solution.py
@@ -63,7 +63,7 @@
             precision=lax.Precision.HIGHEST,
             preferred_element_type=jnp.float32,
         )
-        gram = lax.psum(local_gram, ("row", "vec"))
+        gram = lax.psum(lax.psum(local_gram, axis_name="row"), "vec")
         stacked = 1.5 * stacked - 0.5 * jnp.dot(
             stacked, gram, precision=lax.Precision.HIGHEST, preferred_element_type=jnp.float32
         )

time: 797 us -> 871 us (1.093)
  waiting for transfers between devices: 503 us -> 575 us
    psum x3 -> x6, waiting for transfers between devices: 453 us -> 525 us  [on_device(): gram = lax.psum(lax.psum(local_gram, axis_name='row'), 'vec')]
  transfers between devices with their start and end apart: 7 -> 10, of which waited for: 7 -> 10; matrix products, arithmetic and copies ran while one was open for 0% -> 0% of each run, Pallas kernels for 0% -> 0%
where the time goes in v1:
time: 871 us
  waiting for transfers between devices  575 us (66%)
  blocking collectives  182 us (21%)
  matrix products  71.3 us (8%)
  between operations  15.7 us (2%)
  local copies, waits for them, and re-layouts  13.1 us (2%)
  starting transfers between devices  8.77 us (1%)
    psum x6, waiting for transfers between devices, on_device(): gram = lax.psum(lax.psum(local_gram, axis_name='row'), 'vec')  525 us
    psum x1, blocking collectives, on_device(): energy = lax.psum(jnp.sum(second * second), ('row', 'vec'))  65 us
    all_to_all x3, blocking collectives, on_device(): lax.all_to_all(stacked, 'vec', split_axis=1, concat_axis=0, tiled=True)  60.5 us
    all_to_all x3, blocking collectives, on_device(): lax.all_to_all(current, 'vec', split_axis=0, concat_axis=1, tiled=True)  56.1 us
    ppermute x2, waiting for transfers between devices, with_halo(): lax.ppermute(head, axis, [((i + 1) % count, i) for i in range(count)])  41.4 us
    dot_general x2, matrix products, apply_field(): jnp.einsum('rkij,rkjc->ric', hamiltonian, picked * live_mask[:, :, None,...  38.7 us
  transfers between devices with their start and end apart: 10, of which 10 were waited for; matrix products, arithmetic and copies ran while one was open for 0% of the time, Pallas kernels for 0%

profile of v1, /device:TPU:1, one launch (start us, length us, event | category | flops | bytes accessed | tf_op | source)
XLA Modules:
  0.0 870.8 jit_solution(159823368864319236)
XLA Ops:
  6.5 6.8 collective-permute-start.1
  15.5 20.0 %collective-permute-done.1 = f32[2048,128]{1,0:T(8,128)S(1)} collective-permute-done((f32[2048,128]{1,0:T(8,128)}, f32[2048,128]{1,0:T(8,128)S(1)}, u32[]{:S(2)}, u32[]{:S(2)}) %collective-permute-start.1) | collective-permute-done | bytes 1048608 | tf_op jit(solution)/shard_map/ppermute | solution.py:20
  42.8 5.9 gather_fusion
  48.7 19.3 %fusion.1 = f32[16,128,128,1]{1,2,3,0:T(8,128)S(1)} fusion(f32[16,12,128,128]{3,2,1,0:T(8,128)} %param.9, f32[16,12,128,128]{3,2,1,0:T(8,128)} %bitcast.112, f32[16,12]{1,0:T(8,128)S(1)} %get-tuple-element.10, pred[16,12]{1,0:T(8,128)(4,1)S(1)} %get-tuple-element.8), kind=kOutput, calls=%fused_computation.5 | convolution fusion | flops 4838129664 | bytes 26215360 | tf_op jit(solution)/shard_map/rkij,rkjc->ric/dot_general | solution.py:41
  69.7 21.4 %collective-permute-done.3 = f32[2048,128]{1,0:T(8,128)S(1)} collective-permute-done((f32[2048,128]{1,0:T(8,128)S(1)}, f32[2048,128]{1,0:T(8,128)S(1)}, u32[]{:S(2)}, u32[]{:S(2)}) %collective-permute-start.3) | collective-permute-done | bytes 1048608 | tf_op jit(solution)/shard_map/ppermute | solution.py:20
  95.8 5.9 gather_fusion.1
  101.7 19.4 %fusion = f32[16,128,128,1]{1,2,3,0:T(8,128)S(1)} fusion(f32[16,12,128,128]{3,2,1,0:T(8,128)} %param.9, f32[16,12,128,128]{3,2,1,0:T(8,128)} %bitcast.111, f32[16,12]{1,0:T(8,128)S(1)} %get-tuple-element.10, pred[16,12]{1,0:T(8,128)(4,1)S(1)} %get-tuple-element.8), kind=kOutput, calls=%fused_computation.3 | convolution fusion | flops 4838129664 | bytes 26215360 | tf_op jit(solution)/shard_map/rkij,rkjc->ric/dot_general | solution.py:41
  122.1 65.0 %psum.49 = f32[]{:T(128)} all-reduce(f32[]{:T(128)} %get-tuple-element.6), channel_id=1, replica_groups=mesh['row'=16,'vec'=8] {'row','vec'}, use_global_device_ids=true, to_apply=%region_1.3 | all-reduce | flops 1 | bytes 8 | tf_op jit(solution)/shard_map/psum | solution.py:54
  187.8 19.4 %all_to_all.96 = f32[8,256,128]{2,1,0:T(8,128)S(1)} all-to-all(f32[8,256,128]{2,1,0:T(8,128)S(1)} %bitcast.113), channel_id=1, replica_groups=mesh['row'=16,'vec'=8] {'vec'}, dimensions={0} | all-to-all | bytes 2097152 | tf_op jit(solution)/shard_map/all_to_all | solution.py:58
  207.2 5.1 fusion.21
  212.4 99.5 %all-reduce.7.cloned.1.call-done = f32[1024,1024]{1,0:T(8,128)} async-done(((f32[1024,1024]{1,0:T(8,128)}), f32[1024,1024]{1,0:T(8,128)}) %all-reduce.7.cloned.1.call-update) | async-done | bytes 4194320 | tf_op jit(solution)/shard_map/psum | solution.py:66
  312.0 73.1 %all-reduce.9.cloned.1.call-done = f32[1024,1024]{1,0:T(8,128)} async-done(((f32[1024,1024]{1,0:T(8,128)}), f32[1024,1024]{1,0:T(8,128)}) %all-reduce.9.cloned.1.call-update) | async-done | bytes 4194320 | tf_op jit(solution)/shard_map/psum | solution.py:66
  385.0 5.8 fusion.13
  390.9 20.2 %all_to_all.97 = f32[256,8,128]{2,0,1:T(8,128)S(1)} all-to-all(f32[256,8,128]{2,0,1:T(8,128)S(1)} %bitcast.114), channel_id=1, replica_groups=mesh['row'=16,'vec'=8] {'vec'}, dimensions={1} | all-to-all | bytes 2097152 | tf_op jit(solution)/shard_map/all_to_all | solution.py:70
  411.1 18.4 %all_to_all.98 = f32[8,256,128]{2,1,0:T(8,128)S(1)} all-to-all(f32[8,256,128]{2,1,0:T(8,128)S(1)} %bitcast.115), channel_id=1, replica_groups=mesh['row'=16,'vec'=8] {'vec'}, dimensions={0} | all-to-all | bytes 2097152 | tf_op jit(solution)/shard_map/all_to_all | solution.py:58
  434.6 103.3 %all-reduce.11.cloned.1.call-done = f32[1024,1024]{1,0:T(8,128)} async-done(((f32[1024,1024]{1,0:T(8,128)}), f32[1024,1024]{1,0:T(8,128)}) %all-reduce.11.cloned.1.call-update) | async-done | bytes 4194320 | tf_op jit(solution)/shard_map/psum | solution.py:66
  538.0 72.9 %all-reduce.13.cloned.1.call-done = f32[1024,1024]{1,0:T(8,128)} async-done(((f32[1024,1024]{1,0:T(8,128)}), f32[1024,1024]{1,0:T(8,128)}) %all-reduce.13.cloned.1.call-update) | async-done | bytes 4194320 | tf_op jit(solution)/shard_map/psum | solution.py:66
  610.9 5.8 fusion.11
  616.8 20.2 %all_to_all.99 = f32[256,8,128]{2,0,1:T(8,128)S(1)} all-to-all(f32[256,8,128]{2,0,1:T(8,128)S(1)} %bitcast.116), channel_id=1, replica_groups=mesh['row'=16,'vec'=8] {'vec'}, dimensions={1} | all-to-all | bytes 2097152 | tf_op jit(solution)/shard_map/all_to_all | solution.py:70
  637.0 18.4 %all_to_all.100 = f32[8,256,128]{2,1,0:T(8,128)S(1)} all-to-all(f32[8,256,128]{2,1,0:T(8,128)S(1)} %bitcast.117), channel_id=1, replica_groups=mesh['row'=16,'vec'=8] {'vec'}, dimensions={0} | all-to-all | bytes 2097152 | tf_op jit(solution)/shard_map/all_to_all | solution.py:58
  660.8 103.0 %all-reduce.15.cloned.1.call-done = f32[1024,1024]{1,0:T(8,128)} async-done(((f32[1024,1024]{1,0:T(8,128)}), f32[1024,1024]{1,0:T(8,128)}) %all-reduce.15.cloned.1.call-update) | async-done | bytes 4194320 | tf_op jit(solution)/shard_map/psum | solution.py:66
  763.8 73.0 %all-reduce.17.cloned.1.call-done = f32[1024,1024]{1,0:T(8,128)} async-done(((f32[1024,1024]{1,0:T(8,128)}), f32[1024,1024]{1,0:T(8,128)}) %all-reduce.17.cloned.1.call-update) | async-done | bytes 4194320 | tf_op jit(solution)/shard_map/psum | solution.py:66
  836.8 5.8 fusion.9
  842.7 20.2 %all_to_all.101 = f32[256,8,128]{2,0,1:T(8,128)S(1)} all-to-all(f32[256,8,128]{2,0,1:T(8,128)S(1)} %bitcast.118), channel_id=1, replica_groups=mesh['row'=16,'vec'=8] {'vec'}, dimensions={1} | all-to-all | bytes 2097152 | tf_op jit(solution)/shard_map/all_to_all | solution.py:70
  (41 shorter events, 27.5 us)
Async XLA Ops:
  6.5 305.4 %all-reduce.7.cloned.1.call-start = ((), (), s32[]{:S(2)}) async-start(), calls=%async_computation.6 | async-start | bytes 8388608 | tf_op jit(solution)/shard_map/psum | solution.py:66
  6.5 28.9 %collective-permute-start.1 = (f32[2048,128]{1,0:T(8,128)}, f32[2048,128]{1,0:T(8,128)S(1)}, u32[]{:S(2)}, u32[]{:S(2)}) collective-permute-start(f32[2048,128]{1,0:T(8,128)} %param.8), channel_id=1, source_target_pairs={{8,0},{16,8},{24,16},{32,24},{40,32},{48,40},{56,48},{64,56},{72,6... | collective-permute-start | bytes 3145736 | tf_op jit(solution)/shard_map/ppermute | solution.py:20
  13.3 27.4 %collective-permute-start = (f32[2048,128]{1,0:T(8,128)}, f32[2048,128]{1,0:T(8,128)}, u32[]{:S(2)}, u32[]{:S(2)}) collective-permute-start(f32[2048,128]{1,0:T(8,128)} %param.8), channel_id=1, source_target_pairs={{0,8},{8,16},{16,24},{24,32},{32,40},{40,48},{48,56},{56,64},{64,7... | collective-permute-start | bytes 3145736 | tf_op jit(solution)/shard_map/ppermute | solution.py:18
  35.5 1.0 copy-start.4
  48.7 19.3 %copy-start.2 = (f32[2048,128]{1,0:T(8,128)S(1)}, f32[2048,128]{1,0:T(8,128)}, u32[]{:S(2)}) copy-start(f32[2048,128]{1,0:T(8,128)} %param.8) | copy-start | bytes 3145732
  68.0 27.8 %copy-start = (f32[16,128,128,1]{1,2,3,0:T(8,128)}, f32[16,128,128,1]{1,2,3,0:T(8,128)S(1)}, u32[]{:S(2)}) copy-start(f32[16,128,128,1]{1,2,3,0:T(8,128)S(1)} %fusion.1) | copy-start | bytes 3145732
  68.1 23.0 %collective-permute-start.3 = (f32[2048,128]{1,0:T(8,128)S(1)}, f32[2048,128]{1,0:T(8,128)S(1)}, u32[]{:S(2)}, u32[]{:S(2)}) collective-permute-start(f32[2048,128]{1,0:T(8,128)S(1)} %fusion.26), channel_id=1, source_target_pairs={{8,0},{16,8},{24,16},{32,24},{40,32},{48,40},{56,48},{64,56},{72,6... | collective-permute-start | bytes 3145736 | tf_op jit(solution)/shard_map/ppermute | solution.py:20
  69.4 26.2 %collective-permute-start.2 = (f32[2048,128]{1,0:T(8,128)S(1)}, f32[2048,128]{1,0:T(8,128)S(1)}, u32[]{:S(2)}, u32[]{:S(2)}) collective-permute-start(f32[2048,128]{1,0:T(8,128)S(1)} %fusion.26), channel_id=1, source_target_pairs={{0,8},{8,16},{16,24},{24,32},{32,40},{40,48},{48,56},{56,64},{64,7... | collective-permute-start | bytes 3145736 | tf_op jit(solution)/shard_map/ppermute | solution.py:18
  101.7 19.4 %copy-start.1 = (f32[16,128,128,1]{1,2,3,0:T(8,128)S(1)}, f32[16,128,128,1]{1,2,3,0:T(8,128)}, u32[]{:S(2)}) copy-start(f32[16,128,128,1]{1,2,3,0:T(8,128)} %copy-done) | copy-start | bytes 3145732
  101.7 19.4 %copy-start.3 = (f32[2048,128]{1,0:T(8,128)S(1)}, f32[2048,128]{1,0:T(8,128)}, u32[]{:S(2)}) copy-start(f32[2048,128]{1,0:T(8,128)} %param.8) | copy-start | bytes 3145732
  212.3 172.7 %all-reduce.9.cloned.1.call-start = ((), (), s32[]{:S(2)}) async-start(), calls=%async_computation.7 | async-start | bytes 8388608 | tf_op jit(solution)/shard_map/psum | solution.py:66
  311.9 226.0 %all-reduce.11.cloned.1.call-start = ((), (), s32[]{:S(2)}) async-start(), calls=%async_computation.8 | async-start | bytes 8388608 | tf_op jit(solution)/shard_map/psum | solution.py:66
  434.6 176.3 %all-reduce.13.cloned.1.call-start = ((), (), s32[]{:S(2)}) async-start(), calls=%async_computation.9 | async-start | bytes 8388608 | tf_op jit(solution)/shard_map/psum | solution.py:66
  537.9 225.9 %all-reduce.15.cloned.1.call-start = ((), (), s32[]{:S(2)}) async-start(), calls=%async_computation.10 | async-start | bytes 8388608 | tf_op jit(solution)/shard_map/psum | solution.py:66
  660.4 176.3 %all-reduce.17.cloned.1.call-start = ((), (), s32[]{:S(2)}) async-start(), calls=%async_computation.11 | async-start | bytes 8388608 | tf_op jit(solution)/shard_map/psum | solution.py:66
Sparse Core Ops, SparseCore 0:
  212.4 99.3 all-reduce.6
  314.3 70.7 all-reduce.8
  434.7 103.1 all-reduce.10
  540.1 70.7 all-reduce.12
  660.6 103.1 all-reduce.14
  766.0 70.7 all-reduce.16
